TPU v7x, 32 devices: a whole 2x2x4 slice. The times are simulated.
32 devices in a mesh: dp: 8 (over z, x), seq: 4 (over y, core).
Axes of the slice: x: 2, y: 2, z: 4, core: 2. Of those that a mesh axis runs over, the one named last changes fastest.
Arguments:
- queries: bfloat16 [8, 512, 32, 128], P('dp', 'seq'), may hold values from -13 to 13
- keys: bfloat16 [8, 512, 4, 128], P('dp', 'seq'), may hold values from -13 to 13
- values: bfloat16 [8, 512, 4, 128], P('dp', 'seq'), may hold values from -6 to 6
- d_out: bfloat16 [8, 512, 32, 128], P('dp', 'seq'), may hold values from -6 to 6
- doc_ids: int32 [8, 512], P('dp', 'seq'), may hold values from 0 to 3, never falling along the last dimension, each value on 1 to 256 neighbouring positions
Outputs:
- query_grad: bfloat16 [8, 512, 32, 128], P('dp', 'seq')
- key_grad: bfloat16 [8, 512, 4, 128], P('dp', 'seq')
- value_grad: bfloat16 [8, 512, 4, 128], P('dp', 'seq')
- value_bias_grad: float32 [512], P('dp')
Inputs may be any that keep to these rules, and one draw needn't show every extreme that they name: `doc_ids`: in each row the ids never fall along the tokens; each of the 4 ids marks one document of 1 to 256 tokens, and one document has exactly 256.
All inputs are finite; a program needn't handle non-finite values.
Results may differ from a plain program's by a relative error of at most 0.0073.
Values may be sent and summed in bfloat16 or wider, within the bound.
No kernel may reach another device: no remote copies, remote signals or barrier semaphores. Data moves between devices by JAX's collectives and lax.ppermute only.
A program may use at most 64 MiB of HBM per device.

v0:
```python
import math

import jax
import jax.numpy as jnp
from jax import lax
from jax.sharding import PartitionSpec as P

masked_score = -1e30


def tile_terms(
    query_block,
    grad_block,
    block_of_keys,
    block_of_values,
    query_docs,
    key_docs,
    query_first,
    key_first,
    score_scale,
):
    scores = (
        jnp.einsum("qhd,kd->hqk", query_block, block_of_keys, preferred_element_type=jnp.float32)
        * score_scale
    )
    dweights = jnp.einsum(
        "qhd,kd->hqk", grad_block, block_of_values, preferred_element_type=jnp.float32
    )
    rows_per_block = query_block.shape[0]
    query_place = query_first + jnp.arange(rows_per_block)
    key_place = key_first + jnp.arange(rows_per_block)
    allowed = (key_place[None, :] <= query_place[:, None]) & (
        key_docs[None, :] == query_docs[:, None]
    )
    masked = jnp.where(allowed[None], scores, masked_score)
    return (masked, dweights, allowed)


def shards(queries, keys, values, d_out, doc_ids):
    seq_size = lax.axis_size("seq")
    query_local = queries[0]
    grad_local = d_out[0]
    key_local = keys[0]
    value_local = values[0]
    kv_heads = key_local.shape[1]
    head_dim = key_local.shape[2]
    local_tokens = query_local.shape[0]
    head_copies = seq_size // kv_heads
    documents_per_row = lax.all_gather(doc_ids[0], "seq", axis=0, tiled=True)
    query_row, grad_row = (
        lax.all_to_all(query_local, "seq", split_axis=1, concat_axis=0, tiled=True),
        lax.all_to_all(grad_local, "seq", split_axis=1, concat_axis=0, tiled=True),
    )
    key_copies, value_copies = (
        lax.all_to_all(
            jnp.repeat(key_local, head_copies, axis=1),
            "seq",
            split_axis=1,
            concat_axis=0,
            tiled=True,
        ),
        lax.all_to_all(
            jnp.repeat(value_local, head_copies, axis=1),
            "seq",
            split_axis=1,
            concat_axis=0,
            tiled=True,
        ),
    )
    row_of_keys = key_copies[:, 0]
    row_of_values = value_copies[:, 0]
    row_length = query_row.shape[0]
    local_heads = query_row.shape[1]
    rows_per_block = min(512, row_length)
    block_count = row_length // rows_per_block
    score_scale = 1.0 / math.sqrt(head_dim)
    doc_blocks = documents_per_row.reshape(block_count, rows_per_block)
    lowest = jnp.sum((doc_blocks[None, :, -1] < doc_blocks[:, None, 0]).astype(jnp.int32), axis=1)

    def select_block(array, index):
        return lax.dynamic_slice_in_dim(array, index * rows_per_block, rows_per_block, 0)

    def row_stats(qindex):
        query_block = select_block(query_row, qindex)
        grad_block = select_block(grad_row, qindex)
        query_docs = select_block(documents_per_row, qindex)

        def row_tile_step(key_index, running_total):
            row_top, exp_total, weighted = running_total
            masked, dweights, allowed = tile_terms(
                query_block,
                grad_block,
                select_block(row_of_keys, key_index),
                select_block(row_of_values, key_index),
                query_docs,
                select_block(documents_per_row, key_index),
                qindex * rows_per_block,
                key_index * rows_per_block,
                score_scale,
            )
            new_top = jnp.maximum(row_top, jnp.max(masked, axis=2))
            factor = jnp.exp(row_top - new_top)
            exponent = jnp.where(allowed[None], jnp.exp(masked - new_top[:, :, None]), 0.0)
            return (
                new_top,
                exp_total * factor + jnp.sum(exponent, axis=2),
                weighted * factor + jnp.sum(exponent * dweights, axis=2),
            )

        zeros = jnp.zeros((local_heads, rows_per_block), jnp.float32)
        first_state = (
            jnp.full((local_heads, rows_per_block), masked_score, jnp.float32),
            zeros,
            zeros,
        )
        row_top, exp_total, weighted = lax.fori_loop(
            lowest[qindex], qindex + 1, row_tile_step, first_state
        )
        return (row_top, exp_total, weighted / exp_total)

    row_tops, row_totals, row_deltas = lax.map(row_stats, jnp.arange(block_count))

    def backward(qindex, running_total):
        query_all, key_acc, value_acc = running_total
        query_block = select_block(query_row, qindex)
        grad_block = select_block(grad_row, qindex)
        query_docs = select_block(documents_per_row, qindex)
        row_top = row_tops[qindex]
        exp_total = row_totals[qindex]
        row_delta = row_deltas[qindex]

        def backward_tile_step(key_index, inner_product):
            query_acc, key_inner_product, value_inner_product = inner_product
            block_of_keys = select_block(row_of_keys, key_index)
            block_of_values = select_block(row_of_values, key_index)
            masked, dweights, allowed = tile_terms(
                query_block,
                grad_block,
                block_of_keys,
                block_of_values,
                query_docs,
                select_block(documents_per_row, key_index),
                qindex * rows_per_block,
                key_index * rows_per_block,
                score_scale,
            )
            weights = jnp.where(
                allowed[None], jnp.exp(masked - row_top[:, :, None]) / exp_total[:, :, None], 0.0
            )
            dscores = weights * (dweights - row_delta[:, :, None])
            weights_half = weights.astype(jnp.bfloat16)
            dscores_half = dscores.astype(jnp.bfloat16)
            query_acc = query_acc + jnp.einsum(
                "hqk,kd->qhd", dscores_half, block_of_keys, preferred_element_type=jnp.float32
            )
            key_piece = jnp.einsum(
                "hqk,qhd->kd", dscores_half, query_block, preferred_element_type=jnp.float32
            )
            value_piece = jnp.einsum(
                "hqk,qhd->kd", weights_half, grad_block, preferred_element_type=jnp.float32
            )
            key_inner_product = lax.dynamic_update_slice_in_dim(
                key_inner_product,
                select_block(key_inner_product, key_index) + key_piece,
                key_index * rows_per_block,
                0,
            )
            value_inner_product = lax.dynamic_update_slice_in_dim(
                value_inner_product,
                select_block(value_inner_product, key_index) + value_piece,
                key_index * rows_per_block,
                0,
            )
            return (query_acc, key_inner_product, value_inner_product)

        query_start = jnp.zeros((rows_per_block, local_heads, head_dim), jnp.float32)
        query_acc, key_acc, value_acc = lax.fori_loop(
            lowest[qindex], qindex + 1, backward_tile_step, (query_start, key_acc, value_acc)
        )
        query_all = lax.dynamic_update_slice_in_dim(
            query_all, query_acc, qindex * rows_per_block, 0
        )
        return (query_all, key_acc, value_acc)

    start_state = (
        jnp.zeros((row_length, local_heads, head_dim), jnp.float32),
        jnp.zeros((row_length, head_dim), jnp.float32),
        jnp.zeros((row_length, head_dim), jnp.float32),
    )
    query_all, key_acc, value_acc = lax.fori_loop(0, block_count, backward, start_state)
    query_half = (query_all * score_scale).astype(jnp.bfloat16)
    key_half = (key_acc * score_scale).astype(jnp.bfloat16)[:, None]
    value_half = value_acc.astype(jnp.bfloat16)[:, None]
    query_grad, key_back, value_back = (
        lax.all_to_all(query_half, "seq", split_axis=0, concat_axis=1, tiled=True),
        lax.all_to_all(key_half, "seq", split_axis=0, concat_axis=1, tiled=True),
        lax.all_to_all(value_half, "seq", split_axis=0, concat_axis=1, tiled=True),
    )
    summed_key = jnp.sum(
        key_back.reshape(local_tokens, kv_heads, head_copies, head_dim), axis=2, dtype=jnp.float32
    )
    summed_value = jnp.sum(
        value_back.reshape(local_tokens, kv_heads, head_copies, head_dim), axis=2, dtype=jnp.float32
    )
    partial_value = jnp.sum(summed_value, axis=0).reshape(-1)
    row_bias = lax.psum_scatter(partial_value, "dp", scatter_dimension=0, tiled=True)
    total_bias = lax.psum(row_bias, "seq")
    total_tokens = local_tokens * seq_size * lax.axis_size("dp")
    return (
        query_grad[None],
        summed_key.astype(jnp.bfloat16)[None],
        summed_value.astype(jnp.bfloat16)[None],
        total_bias / math.sqrt(total_tokens),
    )


def solution(mesh):
    placed = (
        P("dp", "seq", None, None),
        P("dp", "seq", None, None),
        P("dp", "seq", None, None),
        P("dp", "seq", None, None),
        P("dp", "seq"),
    )
    return jax.shard_map(
        shards,
        mesh=mesh,
        in_specs=placed,
        out_specs=(
            P("dp", "seq", None, None),
            P("dp", "seq", None, None),
            P("dp", "seq", None, None),
            P("dp"),
        ),
        check_vma=False,
    )
```

profile of v0, /device:TPU:0, one launch (start us, length us, event | category | flops | bytes accessed | tf_op | source)
XLA Modules:
  0.0 128.4 jit_solution(110084953796103875)
XLA Ops:
  0.6 0.0 copy-start.2
  0.6 0.0 copy-start.3
  0.7 1.6 %copy.62 = bf16[1,128,4,128]{3,1,2,0:T(8,128)(2,1)} copy(bf16[1,128,4,128]{3,2,1,0:T(4,128)(2,1)} %param.10) | data formatting | bytes 262144 | tf_op args[1]
  2.3 4.3 %all-to-all-start = ((bf16[128,4,128]{2,0,1:T(8,128)(2,1)}), bf16[128,4,128]{2,0,1:T(8,128)(2,1)S(1)}, u32[]{:S(2)}, u32[]{:S(2)}) async-start(bf16[128,4,128]{2,0,1:T(8,128)(2,1)} %bitcast.125), calls=%async_computation | async-start | bytes 262144 | tf_op jit(solution)/shard_map/all_to_all | solution.py:55
  6.5 2.6 %copy.60 = bf16[1,128,32,128]{3,1,2,0:T(8,128)(2,1)} copy(bf16[1,128,32,128]{3,2,1,0:T(8,128)(2,1)} %param.9) | data formatting | bytes 2097152 | tf_op args[0]
  9.1 2.0 %all-to-all-done = bf16[128,4,128]{2,0,1:T(8,128)(2,1)S(1)} async-done(((bf16[128,4,128]{2,0,1:T(8,128)(2,1)}), bf16[128,4,128]{2,0,1:T(8,128)(2,1)S(1)}, u32[]{:S(2)}, u32[]{:S(2)}) %all-to-all-start) | async-done | bytes 131104 | tf_op jit(solution)/shard_map/all_to_all | solution.py:55
  11.1 3.5 %all-to-all-start.1 = ((bf16[128,32,128]{2,0,1:T(8,128)(2,1)}), bf16[128,32,128]{2,0,1:T(8,128)(2,1)S(1)}, u32[]{:S(2)}, u32[]{:S(2)}) async-start(bf16[128,32,128]{2,0,1:T(8,128)(2,1)} %bitcast.123), calls=%async_computation.1 | async-start | bytes 2097152 | tf_op jit(solution)/shard_map/all_to_all | solution.py:51
  14.7 2.6 %copy.59 = bf16[1,128,32,128]{3,1,2,0:T(8,128)(2,1)} copy(bf16[1,128,32,128]{3,2,1,0:T(8,128)(2,1)} %param.12) | data formatting | bytes 2097152 | tf_op args[3]
  17.3 11.8 %all-to-all-done.1 = bf16[128,32,128]{2,0,1:T(8,128)(2,1)S(1)} async-done(((bf16[128,32,128]{2,0,1:T(8,128)(2,1)}), bf16[128,32,128]{2,0,1:T(8,128)(2,1)S(1)}, u32[]{:S(2)}, u32[]{:S(2)}) %all-to-all-start.1) | async-done | bytes 1048608 | tf_op jit(solution)/shard_map/all_to_all | solution.py:51
  29.1 3.5 %all-to-all-start.3 = ((bf16[128,32,128]{2,0,1:T(8,128)(2,1)}), bf16[128,32,128]{2,0,1:T(8,128)(2,1)S(1)}, u32[]{:S(2)}, u32[]{:S(2)}) async-start(bf16[128,32,128]{2,0,1:T(8,128)(2,1)} %bitcast.122), calls=%async_computation.3 | async-start | bytes 2097152 | tf_op jit(solution)/shard_map/all_to_all | solution.py:52
  32.6 0.0 copy-done.2
  32.6 0.7 copy.61
  33.3 0.0 copy-done.3
  33.3 14.6 %all-gather = s32[1,512]{1,0:T(1,128)S(1)} all-gather(s32[1,128]{1,0:T(1,128)S(1)} %copy-done.3), channel_id=2, replica_groups=mesh['dp'=8,'seq'=4] {'seq'}, dimensions={1}, use_global_device_ids=true | all-gather | bytes 2560 | tf_op jit(solution)/shard_map/all_gather | solution.py:49
  47.9 0.0 all-to-all-done.3
  47.9 3.3 %all-to-all-start.2 = ((bf16[128,4,128]{2,0,1:T(8,128)(2,1)}), bf16[128,4,128]{2,0,1:T(8,128)(2,1)S(1)}, u32[]{:S(2)}, u32[]{:S(2)}) async-start(bf16[128,4,128]{2,0,1:T(8,128)(2,1)} %bitcast.124), calls=%async_computation.2 | async-start | bytes 262144 | tf_op jit(solution)/shard_map/all_to_all | solution.py:62
  51.2 0.6 fusion.28
  53.1 0.1 copy.37
  53.2 0.1 copy.40
  53.3 2.5 %all-to-all-done.2 = bf16[128,4,128]{2,0,1:T(8,128)(2,1)S(1)} async-done(((bf16[128,4,128]{2,0,1:T(8,128)(2,1)}), bf16[128,4,128]{2,0,1:T(8,128)(2,1)S(1)}, u32[]{:S(2)}, u32[]{:S(2)}) %all-to-all-start.2) | async-done | bytes 131104 | tf_op jit(solution)/shard_map/all_to_all | solution.py:62
  55.8 6.9 %while.59 = (s32[]{:T(128)}, f32[8,512]{1,0:T(8,128)S(1)}, f32[8,512]{1,0:T(8,128)S(1)}, f32[8,512]{1,0:T(8,128)S(1)}, s32[512]{0:T(512)S(1)}, /*index=5*/bf16[5...) while((s32[]{:T(128)}, f32[8,512]{1,0:T(8,128)S(1)}, ...), condition=%wide.region_4.0_spmd, body=%wide.region_0.4_spmd.sunk | while | flops 1103901184 | bytes 28874876 | solution.py:116
  55.8 0.3 fusion.62
  56.1 1.5 %fusion.63 = (f32[8,512]{1,0:T(8,128)S(1)}, f32[512,512,8]{1,0,2:T(8,128)S(1)}) fusion(pred[512,512]{0,1:T(8,128)(4,1)S(1)} %fusion.62, bf16[512,8,128]{2,0,1:T(8,128)(2,1)S(1)} %get-tuple-element.748, bf16[512,128]{1,0:T(8,128)(2,1)S(1)} %get-tuple-element.747), kind=kOutput, calls=%fused_computation.4.clone.1 | convolution fusion | flops 543158272 | bytes 9846784 | tf_op jit(solution)/shard_map/while/body/eval_jaxpr/while/body/qhd,kd->hqk/dot_general | solution.py:23
  57.7 2.0 %fusion.65 = f32[8,512]{1,0:T(8,128)S(1)} fusion(f32[512,512,8]{1,0,2:T(8,128)S(1)} %get-tuple-element.705, f32[8,512]{1,0:T(8,128)S(1)} %max.9, pred[512,512]{0,1:T(8,128)(4,1)S(1)} %fusion.62), kind=kLoop, calls=%fused_computation.5.clone.1 | loop fusion | flops 10481664 | bytes 8683520 | tf_op jit(solution)/shard_map/while/body/eval_jaxpr/while/body/reduce_sum | solution.py:106
  59.7 3.0 %fusion.64 = f32[8,512]{1,0:T(8,128)S(1)} fusion(f32[512,512,8]{1,0,2:T(8,128)S(1)} %get-tuple-element.705, f32[8,512]{1,0:T(8,128)S(1)} %max.9, pred[512,512]{0,1:T(8,128)(4,1)S(1)} %fusion.62, bf16[512,8,128]{2,0,1:T(8,128)(2,1)S(1)} %get-tuple-element.750, bf16[512,128]{1,0:T(8,128)(2,1)S(1)} %get-tuple-element.749), kind=kOutput, calls=%fused_computation.1.clone.1 | convolution fusion | flops 549449728 | bytes 9863168 | tf_op jit(solution)/shard_map/while/body/eval_jaxpr/while/body/qhd,kd->hqk/dot_general | solution.py:26
  62.8 1.5 %broadcast.192 = f32[512,8,128]{2,0,1:T(8,128)} broadcast(f32[]{:T(128)} %constant.131.clone.1), dimensions={} | broadcast | bytes 2097156 | tf_op jit(solution)/shard_map/broadcast.14
  64.3 0.0 copy-start.4
  64.3 10.2 %while.60 = (s32[]{:T(128)}, f32[512,8,128]{2,0,1:T(8,128)}, f32[512,128]{1,0:T(8,128)S(1)}, f32[512,128]{1,0:T(8,128)S(1)}, s32[512]{0:T(512)S(1)}, /*index=5*/...) while((s32[]{:T(128)}, f32[512,8,128]{2,0,1:T(8,128)}, ...), condition=%wide.region_6.7_spmd, body=%wide.region_5.0_spmd.sunk | while | flops 2704671232 | bytes 64936140 | solution.py:177
  64.3 0.3 fusion.76
  64.6 2.9 %fusion.77 = f32[8,512,512]{1,2,0:T(8,128)S(1)} fusion(f32[8,512]{1,0:T(8,128)S(1)} %bitcast.190, f32[8,512]{1,0:T(8,128)S(1)} %bitcast.184, pred[512,512]{0,1:T(8,128)(4,1)S(1)} %fusion.76, bf16[512,8,128]{2,0,1:T(8,128)(2,1)S(1)} %get-tuple-element.787, bf16[512,128]{1,0:T(8,128)(2,1)S(1)} %get-tuple-element.786), kind=kOutput, calls=%fused_computation.22.clone.1 | convolution fusion | flops 547356672 | bytes 9863168 | tf_op jit(solution)/shard_map/while/body/eval_jaxpr/while/body/qhd,kd->hqk/dot_general | solution.py:23
  67.5 1.3 %fusion.80 = f32[512,128]{1,0:T(8,128)S(1)} fusion(f32[512,128]{1,0:T(8,128)S(1)} %get-tuple-element.770, bf16[512,8,128]{2,0,1:T(8,128)(2,1)S(1)} %get-tuple-element.791, f32[8,512,512]{1,2,0:T(8,128)S(1)} %fusion.77), kind=kOutput, calls=%fused_computation.28.clone.1 | convolution fusion | flops 539033600 | bytes 9961472 | tf_op jit(solution)/shard_map/while/body/eval_jaxpr/while/body/hqk,qhd->kd/dot_general | solution.py:159
  68.9 0.0 copy-start
  68.9 1.3 %fusion.78 = bf16[8,512,512]{1,2,0:T(8,128)(2,1)S(1)} fusion(f32[8,512,512]{1,2,0:T(8,128)S(1)} %fusion.77, f32[8,512]{1,0:T(8,128)S(1)} %bitcast.191, bf16[512,8,128]{2,0,1:T(8,128)(2,1)S(1)} %get-tuple-element.791, bf16[512,128]{1,0:T(8,128)(2,1)S(1)} %get-tuple-element.790), kind=kOutput, calls=%fused_computation.17.clone.1 | convolution fusion | flops 543162368 | bytes 13778944 | tf_op jit(solution)/shard_map/while/body/eval_jaxpr/while/body/qhd,kd->hqk/dot_general | solution.py:26
  70.2 1.3 fusion.79
  71.5 0.0 copy-done
  71.5 1.7 %bitcast_add_fusion.2 = f32[512,8,128]{2,0,1:T(8,128)S(1)} fusion(f32[512,8,128]{2,0,1:T(8,128)S(1)} %copy-done, bf16[8,512,512]{1,2,0:T(8,128)(2,1)S(1)} %fusion.78, bf16[512,128]{1,0:T(8,128)(2,1)S(1)} %get-tuple-element.786), kind=kOutput, calls=%fused_computation.25.clone.1 | convolution fusion | flops 537395200 | bytes 8519680 | tf_op jit(solution)/shard_map/while/body/eval_jaxpr/while/body/hqk,kd->qhd/dot_general | solution.py:153
  73.1 0.0 copy-start.1
  73.2 1.3 %copy-done.1 = f32[512,8,128]{2,0,1:T(8,128)} copy-done((f32[512,8,128]{2,0,1:T(8,128)}, f32[512,8,128]{2,0,1:T(8,128)S(1)}, u32[]{:S(2)}) %copy-start.1) | copy-done | bytes 2097176 | tf_op jit(solution)/shard_map/while/body/eval_jaxpr/while
  74.5 0.5 broadcast.200
  75.1 0.7 reduce.1
  75.7 0.7 reshape.211
  76.4 3.3 %all-to-all-start.5 = ((bf16[4,2,8192]{2,1,0:T(2,128)(2,1)}), bf16[4,2,8192]{2,1,0:T(2,128)(2,1)S(1)}, u32[]{:S(2)}, u32[]{:S(2)}) async-start(bf16[4,2,8192]{2,1,0:T(2,128)(2,1)} %reshape.211), calls=%async_computation.5 | async-start | bytes 262144 | tf_op jit(solution)/shard_map/all_to_all | solution.py:196
  79.8 0.7 reduce.2
  80.4 0.7 reshape.213
  81.1 3.2 %all-to-all-done.5 = bf16[4,2,8192]{2,1,0:T(2,128)(2,1)S(1)} async-done(((bf16[4,2,8192]{2,1,0:T(2,128)(2,1)}), bf16[4,2,8192]{2,1,0:T(2,128)(2,1)S(1)}, u32[]{:S(2)}, u32[]{:S(2)}) %all-to-all-start.5) | async-done | bytes 131104 | tf_op jit(solution)/shard_map/all_to_all | solution.py:196
  84.3 3.3 %all-to-all-start.6 = ((bf16[4,2,8192]{2,1,0:T(2,128)(2,1)}), bf16[4,2,8192]{2,1,0:T(2,128)(2,1)S(1)}, u32[]{:S(2)}, u32[]{:S(2)}) async-start(bf16[4,2,8192]{2,1,0:T(2,128)(2,1)} %reshape.213), calls=%async_computation.6 | async-start | bytes 262144 | tf_op jit(solution)/shard_map/all_to_all | solution.py:197
  87.7 3.9 %fusion.26 = bf16[512,8,128]{2,1,0:T(8,128)(2,1)} fusion(f32[512,8,128]{2,0,1:T(8,128)} %get-tuple-element.519), kind=kLoop, calls=%fused_computation.37 | loop fusion | flops 1048576 | bytes 3145728 | tf_op jit(solution)/shard_map/convert_element_type | solution.py:191
  91.6 0.7 all-to-all-done.6
  92.2 3.5 %all-to-all-start.4 = ((bf16[512,8,128]{2,1,0:T(8,128)(2,1)}), bf16[512,8,128]{2,1,0:T(8,128)(2,1)S(1)}, u32[]{:S(2)}, u32[]{:S(2)}) async-start(bf16[512,8,128]{2,1,0:T(8,128)(2,1)} %fusion.26), calls=%async_computation.4 | async-start | bytes 2097152 | tf_op jit(solution)/shard_map/all_to_all | solution.py:195
  95.8 0.0 copy-done.4
  95.8 0.6 dynamic-slice.3
  97.0 0.1 reshape.214
  97.2 0.8 copy.46
  97.9 0.1 reshape.212
  98.1 0.8 copy.45
  98.9 22.1 %all-reduce = f32[512]{0:T(512)S(1)} all-reduce(f32[512]{0:T(512)S(1)} %bitcast.193), channel_id=3, replica_groups=mesh['dp'=8,'seq'=4] {'dp'}, use_global_device_ids=true, to_apply=%region_8.9.clone | all-reduce | flops 512 | bytes 4096
  121.0 0.1 dynamic-slice.4
  121.1 5.6 %psum.7 = f32[64]{0:T(128)S(1)} all-reduce(f32[64]{0:T(128)S(1)} %dynamic-slice.4), channel_id=1, replica_groups=mesh['dp'=8,'seq'=4] {'seq'}, use_global_device_ids=true, to_apply=%region_9.10 | all-reduce | flops 64 | bytes 512 | tf_op jit(solution)/shard_map/psum | solution.py:207
  126.7 0.5 broadcast_multiply_fusion
  127.2 0.0 all-to-all-done.4
  127.2 1.2 copy.58
  (15 shorter events, 0.2 us)
Async XLA Ops:
  0.6 31.9 %copy-start.2 = (bf16[1,128,4,128]{3,2,1,0:T(4,128)(2,1)S(1)}, bf16[1,128,4,128]{3,2,1,0:T(4,128)(2,1)}, u32[]{:S(2)}) copy-start(bf16[1,128,4,128]{3,2,1,0:T(4,128)(2,1)} %param.11) | copy-start | bytes 393220
  0.6 32.6 %copy-start.3 = (s32[1,128]{1,0:T(1,128)S(1)}, s32[1,128]{1,0:T(1,128)}, u32[]{:S(2)}) copy-start(s32[1,128]{1,0:T(1,128)} %param.13) | copy-start | bytes 1540
  2.3 8.9 %all-to-all-start = ((bf16[128,4,128]{2,0,1:T(8,128)(2,1)}), bf16[128,4,128]{2,0,1:T(8,128)(2,1)S(1)}, u32[]{:S(2)}, u32[]{:S(2)}) async-start(bf16[128,4,128]{2,0,1:T(8,128)(2,1)} %bitcast.125), calls=%async_computation | async-start | bytes 262144 | tf_op jit(solution)/shard_map/all_to_all | solution.py:55
  11.1 17.9 %all-to-all-start.1 = ((bf16[128,32,128]{2,0,1:T(8,128)(2,1)}), bf16[128,32,128]{2,0,1:T(8,128)(2,1)S(1)}, u32[]{:S(2)}, u32[]{:S(2)}) async-start(bf16[128,32,128]{2,0,1:T(8,128)(2,1)} %bitcast.123), calls=%async_computation.1 | async-start | bytes 2097152 | tf_op jit(solution)/shard_map/all_to_all | solution.py:51
  29.1 18.8 %all-to-all-start.3 = ((bf16[128,32,128]{2,0,1:T(8,128)(2,1)}), bf16[128,32,128]{2,0,1:T(8,128)(2,1)S(1)}, u32[]{:S(2)}, u32[]{:S(2)}) async-start(bf16[128,32,128]{2,0,1:T(8,128)(2,1)} %bitcast.122), calls=%async_computation.3 | async-start | bytes 2097152 | tf_op jit(solution)/shard_map/all_to_all | solution.py:52
  47.9 7.9 %all-to-all-start.2 = ((bf16[128,4,128]{2,0,1:T(8,128)(2,1)}), bf16[128,4,128]{2,0,1:T(8,128)(2,1)S(1)}, u32[]{:S(2)}, u32[]{:S(2)}) async-start(bf16[128,4,128]{2,0,1:T(8,128)(2,1)} %bitcast.124), calls=%async_computation.2 | async-start | bytes 262144 | tf_op jit(solution)/shard_map/all_to_all | solution.py:62
  64.3 31.4 %copy-start.4 = (u32[32]{0:T(128)S(1)}, u32[32]{0:T(128)}, u32[]{:S(2)}) copy-start(u32[32]{0:T(128)} %constant.142) | copy-start | bytes 388
  68.9 2.6 %copy-start = (f32[512,8,128]{2,0,1:T(8,128)S(1)}, f32[512,8,128]{2,0,1:T(8,128)}, u32[]{:S(2)}) copy-start(f32[512,8,128]{2,0,1:T(8,128)} %get-tuple-element.768) | copy-start | bytes 6291460 | tf_op jit(solution)/shard_map/while/body/eval_jaxpr/while
  73.1 1.3 %copy-start.1 = (f32[512,8,128]{2,0,1:T(8,128)}, f32[512,8,128]{2,0,1:T(8,128)S(1)}, u32[]{:S(2)}) copy-start(f32[512,8,128]{2,0,1:T(8,128)S(1)} %bitcast_add_fusion.2) | copy-start | bytes 6291460 | tf_op jit(solution)/shard_map/while/body/eval_jaxpr/while
  76.4 7.9 %all-to-all-start.5 = ((bf16[4,2,8192]{2,1,0:T(2,128)(2,1)}), bf16[4,2,8192]{2,1,0:T(2,128)(2,1)S(1)}, u32[]{:S(2)}, u32[]{:S(2)}) async-start(bf16[4,2,8192]{2,1,0:T(2,128)(2,1)} %reshape.211), calls=%async_computation.5 | async-start | bytes 262144 | tf_op jit(solution)/shard_map/all_to_all | solution.py:196
  84.3 7.9 %all-to-all-start.6 = ((bf16[4,2,8192]{2,1,0:T(2,128)(2,1)}), bf16[4,2,8192]{2,1,0:T(2,128)(2,1)S(1)}, u32[]{:S(2)}, u32[]{:S(2)}) async-start(bf16[4,2,8192]{2,1,0:T(2,128)(2,1)} %reshape.213), calls=%async_computation.6 | async-start | bytes 262144 | tf_op jit(solution)/shard_map/all_to_all | solution.py:197
  92.2 35.0 %all-to-all-start.4 = ((bf16[512,8,128]{2,1,0:T(8,128)(2,1)}), bf16[512,8,128]{2,1,0:T(8,128)(2,1)S(1)}, u32[]{:S(2)}, u32[]{:S(2)}) async-start(bf16[512,8,128]{2,1,0:T(8,128)(2,1)} %fusion.26), calls=%async_computation.4 | async-start | bytes 2097152 | tf_op jit(solution)/shard_map/all_to_all | solution.py:195
where the time goes:
time: 129 us; the launch traced here: 128 us
  blocking collectives  42.4 us (33%)
  starting transfers between devices  24.8 us (19%)
  waiting for transfers between devices  20.1 us (16%)
  local copies, waits for them, and re-layouts  16.7 us (13%)
  matrix products  13 us (10%)
  other arithmetic  8.5 us (7%)
  between operations  2.77 us (2%)
    unnamed x1, blocking collectives  22.1 us
    all_gather x1, blocking collectives, shards(): documents_per_row = lax.all_gather(doc_ids[0], 'seq', axis=0, tiled=True)  14.6 us
    all_to_all x1, waiting for transfers between devices, shards(): lax.all_to_all(query_local, 'seq', split_axis=1, concat_axis=0, tiled=True)  11.8 us
    unnamed x20, local copies, waits for them, and re-layouts  11.4 us
    psum x1, blocking collectives, shards(): total_bias = lax.psum(row_bias, 'seq')  5.63 us
    dot_general x2, matrix products, tile_terms(): jnp.einsum('qhd,kd->hqk', query_block, block_of_keys, preferred_element_t...  4.44 us
    dot_general x2, matrix products, tile_terms(): jnp.einsum('qhd,kd->hqk', grad_block, block_of_values, preferred_element_...  4.28 us
    all_to_all x1, starting transfers between devices, shards(): lax.all_to_all(jnp.repeat(key_local, head_copies, axis=1), 'seq', split_a...  4.26 us
  transfers between devices with their start and end apart: 7, of which 5 were waited for; matrix products, arithmetic and copies ran while one was open for 12% of the time, Pallas kernels for 0%

commit v1 on v0

v1 whole, which is shorter than its diff:
```python
import functools
import math

import jax
import jax.numpy as jnp
from jax import lax
from jax.experimental import pallas as pl
from jax.experimental.pallas import tpu as pltpu
from jax.sharding import PartitionSpec as P

masked_score = -1e30
rows_of_tile = 8


def dot(left, right, left_axis, right_axis):
    return lax.dot_general(
        left, right, (((left_axis,), (right_axis,)), ((), ())), preferred_element_type=jnp.float32
    )


def pick_head(head, tokens, heads):
    row = lax.broadcasted_iota(jnp.int32, (tokens, tokens * heads), 0)
    column = lax.broadcasted_iota(jnp.int32, (tokens, tokens * heads), 1)
    return (column == row * heads + head).astype(jnp.bfloat16)


def attention_kernel(near_count, score_scale, *refs):
    (place_ref, own_docs, near_docs, far_docs, queries, grads, key_refs, value_refs) = (
        refs[0],
        refs[1],
        refs[2 : 2 + near_count],
        refs[2 + near_count],
        refs[3 + near_count],
        refs[4 + near_count],
        refs[5 + near_count : 7 + 2 * near_count],
        refs[7 + 2 * near_count : 9 + 3 * near_count],
    )
    rest = refs[9 + 3 * near_count :]
    query_out, key_out, value_out, key_rows, value_rows, bias = rest
    group = pl.program_id(0)
    tokens, group_heads, head_dim = queries.shape
    chunks = near_count + 2
    heads = key_rows.shape[0]
    block = max(tokens // 4, 16)
    blocks = tokens // block
    rows = block * group_heads
    span = (near_count + 1) * tokens + block

    @pl.when(group == 0)
    def _():
        place = place_ref[0]
        for head in range(heads):
            chosen = pick_head(head, tokens, heads)
            for at in range(chunks):
                into = pl.ds(at * tokens, tokens)
                key_rows[head, into, :] = dot(chosen, key_refs[at][...], 1, 0).astype(jnp.bfloat16)
                value_rows[head, into, :] = dot(chosen, value_refs[at][...], 1, 0).astype(
                    jnp.bfloat16
                )
        own = own_docs[...]
        all_docs = jnp.concatenate([far_docs[...]] + [d[...] for d in near_docs] + [own], axis=1)
        key_ids = jnp.transpose(
            jnp.broadcast_to(all_docs.astype(jnp.float32), (rows_of_tile, chunks * tokens))
        )[:, :1]
        own_ids = jnp.broadcast_to(own.astype(jnp.float32), (rows_of_tile, tokens)).astype(
            jnp.bfloat16
        )
        for at in range(blocks):
            token = lax.broadcasted_iota(jnp.int32, (tokens, rows), 0)
            lane = lax.broadcasted_iota(jnp.int32, (tokens, rows), 1)
            spread = (token == at * block + lane // group_heads).astype(jnp.bfloat16)
            query_ids = dot(own_ids, spread, 1, 0)[:1]
            key_place = at * block + lax.broadcasted_iota(jnp.int32, (span, rows), 0)
            query_place = (
                (chunks - 1) * tokens
                + at * block
                + lax.broadcasted_iota(jnp.int32, (span, rows), 1) // group_heads
            )
            allowed = (
                (key_place <= query_place)
                & (key_place >= (chunks - 1 - place) * tokens)
                & (key_ids[at * block : at * block + span] == query_ids)
            )
            bias[at] = jnp.where(allowed, 0.0, masked_score)

    key_out[...] = jnp.zeros_like(key_out)
    value_out[...] = jnp.zeros_like(value_out)
    for at in range(blocks):
        some = slice(at * block, (at + 1) * block)
        keys_at = pl.ds(at * block, span)
        query = queries[some].reshape(rows, head_dim)
        grad = grads[some].reshape(rows, head_dim)
        key = key_rows[group, keys_at, :]
        value = value_rows[group, keys_at, :]
        scores = dot(key, query, 1, 1) * (score_scale * math.log2(math.e)) + bias[at]
        exponent = jnp.exp2(scores - jnp.max(scores, axis=0, keepdims=True))
        weights = exponent * (1.0 / jnp.sum(exponent, axis=0, keepdims=True))
        dweights = dot(value, grad, 1, 1)
        row_delta = jnp.sum(weights * dweights, axis=0, keepdims=True)
        dscores = (weights * (dweights - row_delta)).astype(jnp.bfloat16)
        value_out[0, keys_at, :] += dot(weights.astype(jnp.bfloat16), grad, 1, 0)
        key_out[0, keys_at, :] += dot(dscores, query, 1, 0)
        query_grad = dot(dscores, key, 0, 0) * score_scale
        query_out[some] = query_grad.astype(jnp.bfloat16).reshape(block, group_heads, head_dim)
    key_out[...] = key_out[...] * score_scale


def attention(place, docs, queries, grads, keys, values, kv_heads, score_scale):
    tokens, heads, head_dim = queries.shape
    chunks = len(keys)
    near = chunks - 2
    group_heads = heads // kv_heads
    block = max(tokens // 4, 16)
    span = (near + 1) * tokens + block
    head_block = pl.BlockSpec((tokens, group_heads, head_dim), lambda g: (0, g, 0))
    sum_block = pl.BlockSpec((1, chunks * tokens, head_dim), lambda g: (g, 0, 0))
    vmem = pl.BlockSpec(memory_space=pltpu.VMEM)
    sums = jax.ShapeDtypeStruct((kv_heads, chunks * tokens, head_dim), jnp.float32)
    return pl.pallas_call(
        functools.partial(attention_kernel, near, score_scale),
        out_shape=(jax.ShapeDtypeStruct(queries.shape, jnp.bfloat16), sums, sums),
        grid=(kv_heads,),
        in_specs=[pl.BlockSpec(memory_space=pltpu.SMEM)]
        + [vmem] * chunks
        + [head_block, head_block]
        + [vmem] * (2 * chunks),
        out_specs=(head_block, sum_block, sum_block),
        scratch_shapes=[
            pltpu.VMEM((kv_heads, chunks * tokens, head_dim), jnp.bfloat16),
            pltpu.VMEM((kv_heads, chunks * tokens, head_dim), jnp.bfloat16),
            pltpu.VMEM((tokens // block, span, block * group_heads), jnp.float32),
        ],
        name="attention",
    )(place, docs[-1], *docs[1:-1], docs[0], queries, grads, *keys, *values)


def finish_kernel(kv_heads, *refs):
    own_key, own_value, key_more, value_more, key_out, value_out = refs
    tokens = own_key.shape[1]
    for own, more, out in ((own_key, key_more, key_out), (own_value, value_more, value_out)):
        total = None
        for head in range(kv_heads):
            half = (own[head] + more[head].astype(jnp.float32)).astype(jnp.bfloat16)
            placed = dot(pick_head(head, tokens, kv_heads), half, 0, 0)
            total = placed if total is None else total + placed
        out[...] = total.astype(jnp.bfloat16)


def shards(queries, keys, values, d_out, doc_ids):
    seq_size = lax.axis_size("seq")
    place = lax.axis_index("seq")
    tokens, kv_heads, head_dim = keys.shape[1:]
    heads = queries.shape[2]
    halo = seq_size // 2
    score_scale = 1.0 / math.sqrt(head_dim)
    key_local = keys.reshape(tokens * kv_heads, head_dim)
    value_local = values.reshape(tokens * kv_heads, head_dim)

    def swap(array, distance):
        pairs = [(i, i ^ distance) for i in range(seq_size)]
        return lax.ppermute(array, "seq", pairs)

    def shift(array, distance):
        pairs = [(i, (i + distance) % seq_size) for i in range(seq_size)]
        return lax.ppermute(array, "seq", pairs)

    odd = place % 2 == 1
    if halo == 2:
        def fetch(array):
            beside, far = swap(array, 1), swap(array, 2)
            return (far, jnp.where(odd, beside, swap(far, 1)), array)
    else:
        def fetch(array):
            return tuple(shift(array, d) for d in range(halo, 0, -1)) + (array,)

    docs, key_all, value_all = fetch(doc_ids), fetch(key_local), fetch(value_local)
    query_grad, key_sums, value_sums = attention(
        place.reshape(1), docs, queries[0], d_out[0], key_all, value_all, kv_heads, score_scale
    )

    def part(array, at):
        return array[:, at * tokens : (at + 1) * tokens]

    def give_back(sums):
        own, far = part(sums, halo), part(sums, 0)
        if halo == 2:
            got = swap(part(sums, 1).astype(jnp.bfloat16), 1).astype(jnp.float32)
            got_far = jnp.where(odd, got, 0.0)
            own = own + jnp.where(odd, 0.0, got)
            more = swap((far + got_far).astype(jnp.bfloat16), 2)
            return (own, more)
        more = 0.0
        for at in range(halo):
            back = shift(part(sums, at).astype(jnp.bfloat16), at - halo).astype(jnp.float32)
            more = more + jnp.where(place < seq_size - halo + at, back, 0.0)
        return (own, more)

    own_value, value_more = give_back(value_sums)
    own_key, key_more = give_back(key_sums)
    flat = jax.ShapeDtypeStruct((tokens * kv_heads, head_dim), jnp.bfloat16)
    key_grad, value_grad = pl.pallas_call(
        functools.partial(finish_kernel, kv_heads), out_shape=(flat, flat), name="finish"
    )(own_key, own_value, key_more, value_more)

    bias = jnp.sum(
        d_out[0].astype(jnp.float32).reshape(tokens, kv_heads, heads // kv_heads, head_dim), (0, 2)
    )
    total_tokens = tokens * seq_size
    for axis in ("seq", "dp"):
        size = lax.axis_size(axis)
        step = 1
        while step < size:
            bias = bias + lax.ppermute(bias, axis, [(i, i ^ step) for i in range(size)])
            step *= 2
    dp_size = lax.axis_size("dp")
    total_tokens = total_tokens * dp_size
    width = kv_heads * head_dim // dp_size
    bias = lax.dynamic_slice_in_dim(bias.reshape(-1), lax.axis_index("dp") * width, width)
    return (
        query_grad[None],
        key_grad.reshape(keys.shape),
        value_grad.reshape(values.shape),
        bias / math.sqrt(total_tokens),
    )


def solution(mesh):
    placed = P("dp", "seq", None, None)
    return jax.shard_map(
        shards,
        mesh=mesh,
        in_specs=(placed, placed, placed, placed, P("dp", "seq")),
        out_specs=(placed, placed, placed, P("dp")),
        check_vma=False,
    )
```

time: 129 us -> 52.7 us (0.41)
  blocking collectives: 42.4 us -> 0 us
  local copies, waits for them, and re-layouts: 16.7 us -> 1.79 us
  Pallas kernels: 0 us -> 13.6 us
  matrix products: 13 us -> 0 us
  starting transfers between devices: 24.8 us -> 16.7 us
  waiting for transfers between devices: 20.1 us -> 15.3 us
  other arithmetic: 8.5 us -> 4.29 us
  between operations: 2.77 us -> 0.73 us
    all_to_all x7 -> x0, starting transfers between devices: 24.8 us -> none  [the longest x1 4.26 us: shards(): lax.all_to_all(jnp.repeat(key_local, head_copies, axis=1), 'seq', split_a...]
    unnamed x1 -> x0, blocking collectives: 22.1 us -> none
    all_to_all x7 -> x0, waiting for transfers between devices: 20.1 us -> none  [the longest x1 11.8 us: shards(): lax.all_to_all(query_local, 'seq', split_axis=1, concat_axis=0, tiled=True)]
    ppermute x0 -> x18, starting transfers between devices: none -> 16.7 us  [the longest x5 8.48 us: shards(): bias = bias + lax.ppermute(bias, axis, [(i, i ^ step) for i in range(size)])]
    ppermute x0 -> x18, waiting for transfers between devices: none -> 15.3 us  [the longest x13 9 us: swap(): return lax.ppermute(array, 'seq', pairs)]
    all_gather x1 -> x0, blocking collectives: 14.6 us -> none  [shards(): documents_per_row = lax.all_gather(doc_ids[0], 'seq', axis=0, tiled=True)]
    pallas_call x0 -> x2, Pallas kernels: none -> 13.6 us  [the longest x1 11.4 us: attention(): pl.pallas_call(functools.partial(attention_kernel, near, score_scale), ou...]
    dot_general x7 -> x0, matrix products: 13 us -> none  [the longest x2 4.44 us: tile_terms(): jnp.einsum('qhd,kd->hqk', query_block, block_of_keys, preferred_element_t...]
  transfers between devices with their start and end apart: 7 -> 18, of which waited for: 5 -> 10; matrix products, arithmetic and copies ran while one was open for 12% -> 7% of each run, Pallas kernels for 0% -> 0%
where the time goes in v1:
time: 52.7 us; the launch traced here: 52.5 us
  starting transfers between devices  16.7 us (32%)
  waiting for transfers between devices  15.3 us (29%)
  Pallas kernels  13.6 us (26%)
  other arithmetic  4.29 us (8%)
  local copies, waits for them, and re-layouts  1.79 us (3%)
  between operations  0.73 us (1%)
    pallas_call x1, Pallas kernels, attention(): pl.pallas_call(functools.partial(attention_kernel, near, score_scale), ou...  11.4 us
    ppermute x13, waiting for transfers between devices, swap(): return lax.ppermute(array, 'seq', pairs)  9 us
    ppermute x5, starting transfers between devices, shards(): bias = bias + lax.ppermute(bias, axis, [(i, i ^ step) for i in range(size)])  8.48 us
    ppermute x13, starting transfers between devices, swap(): return lax.ppermute(array, 'seq', pairs)  8.25 us
    ppermute x5, waiting for transfers between devices, shards(): bias = bias + lax.ppermute(bias, axis, [(i, i ^ step) for i in range(size)])  6.33 us
    pallas_call x1, Pallas kernels, shards(): pl.pallas_call(functools.partial(finish_kernel, kv_heads), out_shape=(fla...  2.27 us
    select_n x3, other arithmetic, fetch(): return (far, jnp.where(odd, beside, swap(far, 1)), array)  1.94 us
    convert_element_type x2, other arithmetic, give_back(): more = swap((far + got_far).astype(jnp.bfloat16), 2)  1.53 us
  transfers between devices with their start and end apart: 18, of which 10 were waited for; matrix products, arithmetic and copies ran while one was open for 7% of the time, Pallas kernels for 0%

profile of v1, /device:TPU:0, one launch (start us, length us, event | category | flops | bytes accessed | tf_op | source)
XLA Modules:
  0.0 52.5 jit_solution(5484185134211078464)
XLA Ops:
  0.6 3.1 %collective-permute-start.6 = (bf16[512,128]{1,0:T(8,128)(2,1)}, bf16[512,128]{1,0:T(8,128)(2,1)S(1)}, u32[]{:S(2)}, u32[]{:S(2)}) collective-permute-start(bf16[512,128]{1,0:T(8,128)(2,1)} %bitcast.17), channel_id=1, source_target_pairs={{0,2},{1,3},{2,0},{3,1},{4,6},{5,7},{6,4},{7,5},{8,10},{9,11},{10,... | collective-permute-start | bytes 393224 | tf_op jit(solution)/shard_map/ppermute | solution.py:161
  3.7 0.0 collective-permute-start.7
  3.7 0.2 collective-permute-start.1
  3.9 0.4 collective-permute-start
  4.2 1.7 %collective-permute-start.3 = (bf16[512,128]{1,0:T(8,128)(2,1)}, bf16[512,128]{1,0:T(8,128)(2,1)S(1)}, u32[]{:S(2)}, u32[]{:S(2)}) collective-permute-start(bf16[512,128]{1,0:T(8,128)(2,1)} %bitcast.14), channel_id=1, source_target_pairs={{0,2},{1,3},{2,0},{3,1},{4,6},{5,7},{6,4},{7,5},{8,10},{9,11},{10,... | collective-permute-start | bytes 393224 | tf_op jit(solution)/shard_map/ppermute | solution.py:161
  5.9 1.7 %collective-permute-done.1.refs_3_ = s32[1,128]{1,0:T(1,128)S(1)} collective-permute-done((s32[1,128]{1,0:T(1,128)}, s32[1,128]{1,0:T(1,128)S(1)}, u32[]{:S(2)}, u32[]{:S(2)}) %collective-permute-start.1) | collective-permute-done | bytes 544 | tf_op jit(solution)/shard_map/ppermute | solution.py:161
  7.6 0.0 copy-start.7
  7.6 0.0 collective-permute-start.2
  7.6 0.0 collective-permute-done
  7.6 0.5 collective-permute-start.4
  8.1 0.0 collective-permute-done.6.refs_9_
  8.1 0.0 copy-start.3
  8.1 0.1 collective-permute-start.8
  8.2 0.6 %collective-permute-done.2 = s32[1,128]{1,0:T(1,128)S(1)} collective-permute-done((s32[1,128]{1,0:T(1,128)S(1)}, s32[1,128]{1,0:T(1,128)S(1)}, u32[]{:S(2)}, u32[]{:S(2)}) %collective-permute-start.2) | collective-permute-done | bytes 544 | tf_op jit(solution)/shard_map/ppermute | solution.py:161
  8.8 0.6 %broadcast_select_fusion.2.refs_2_ = s32[1,128]{1,0:T(1,128)} fusion(s32[1,128]{1,0:T(1,128)S(1)} %collective-permute-done, s32[1,128]{1,0:T(1,128)S(1)} %collective-permute-done.2, pred[]{:T(512)S(6)} %eq.5), kind=kLoop, calls=%fused_computation.17 | loop fusion | flops 128 | bytes 1537 | tf_op jit(solution)/shard_map/jit(_where)/select_n | solution.py:171
  9.4 0.9 %collective-permute-done.3.refs_6_ = bf16[512,128]{1,0:T(8,128)(2,1)S(1)} collective-permute-done((bf16[512,128]{1,0:T(8,128)(2,1)}, bf16[512,128]{1,0:T(8,128)(2,1)S(1)}, u32[]{:S(2)}, u32[]{:S(2)}) %collective-permute-start.3) | collective-permute-done | bytes 131104 | tf_op jit(solution)/shard_map/ppermute | solution.py:161
  10.2 0.0 copy-start.4
  10.2 0.0 collective-permute-start.5
  10.2 0.0 collective-permute-done.7
  10.2 0.0 collective-permute-done.8
  10.2 0.7 %broadcast_select_fusion.refs_10_ = bf16[512,128]{1,0:T(8,128)(2,1)} fusion(bf16[512,128]{1,0:T(8,128)(2,1)S(1)} %collective-permute-done.7, bf16[512,128]{1,0:T(8,128)(2,1)S(1)} %collective-permute-done.8, pred[]{:T(512)S(6)} %eq.5), kind=kLoop, calls=%fused_computation.13 | loop fusion | flops 65536 | bytes 393217 | tf_op jit(solution)/shard_map/jit(_where)/select_n | solution.py:171
  10.9 0.0 collective-permute-done.4
  10.9 0.6 %collective-permute-done.5 = bf16[512,128]{1,0:T(8,128)(2,1)S(1)} collective-permute-done((bf16[512,128]{1,0:T(8,128)(2,1)S(1)}, bf16[512,128]{1,0:T(8,128)(2,1)S(1)}, u32[]{:S(2)}, u32[]{:S(2)}) %collective-permute-start.5) | collective-permute-done | bytes 131104 | tf_op jit(solution)/shard_map/ppermute | solution.py:161
  11.6 0.7 %broadcast_select_fusion.1.refs_7_ = bf16[512,128]{1,0:T(8,128)(2,1)} fusion(bf16[512,128]{1,0:T(8,128)(2,1)S(1)} %collective-permute-done.4, bf16[512,128]{1,0:T(8,128)(2,1)S(1)} %collective-permute-done.5, pred[]{:T(512)S(6)} %eq.5), kind=kLoop, calls=%fused_computation.14 | loop fusion | flops 65536 | bytes 393217 | tf_op jit(solution)/shard_map/jit(_where)/select_n | solution.py:171
  12.2 0.0 copy-done.7
  12.2 0.0 copy-done.3
  12.2 0.0 copy-done.4
  12.2 0.0 copy-start
  12.3 11.4 %attention.1 = (bf16[128,32,128]{2,1,0:T(8,128)(2,1)}, f32[4,384,128]{2,1,0:T(8,128)}, f32[4,384,128]{2,1,0:T(8,128)}) custom-call(s32[1]{0:T(128)} %bitcast.refs_0_, s32[1,128]{1,0:T(1,128)} %refs_1_.1, s32[1,128]{1,0:T(1,128)} %broadcast_select_fusion.2.refs_2_, s32[1,128]{1,0:T(1,128)} %copy-done.7, bf16[128,32,128]{2,1,0:T(8,128)(2,1)} %bitcast.13, ...), custom_call_target="tpu_custom_call" | custom-call | tf_op jit(solution)/shard_map/attention/pallas_call | solution.py:119
  23.6 0.0 copy-start.1
  23.6 0.0 copy-start.2
  23.7 1.1 %slice.34 = bf16[4,128,128]{2,1,0:T(8,128)(2,1)S(1)} slice(f32[4,384,128]{2,1,0:T(8,128)} %get-tuple-element.11), slice={[0:4], [128:256], [0:128]} | slice | bytes 262144 | tf_op jit(solution)/shard_map/slice | solution.py:182
  24.7 0.2 collective-permute-start.10
  25.0 0.0 copy-done
  25.0 0.2 convert_reduce_fusion
  25.2 0.4 collective-permute-start.13
  25.6 0.8 %collective-permute-done.13 = f32[4,128]{1,0:T(4,128)S(1)} collective-permute-done((f32[4,128]{1,0:T(4,128)S(1)}, f32[4,128]{1,0:T(4,128)S(1)}, u32[]{:S(2)}, u32[]{:S(2)}) %collective-permute-start.13) | collective-permute-done | bytes 2080 | tf_op jit(solution)/shard_map/ppermute | solution.py:213
  26.4 1.7 %collective-permute-start.14 = (f32[4,128]{1,0:T(4,128)S(1)}, f32[4,128]{1,0:T(4,128)S(1)}, u32[]{:S(2)}, u32[]{:S(2)}) collective-permute-start(f32[4,128]{1,0:T(4,128)S(1)} %add.39), channel_id=1, source_target_pairs={{0,2},{1,3},{2,0},{3,1},{4,6},{5,7},{6,4},{7,5},{8,10},{9,11},{10,... | collective-permute-start | bytes 6152 | tf_op jit(solution)/shard_map/ppermute | solution.py:213
  28.2 1.8 %collective-permute-done.14 = f32[4,128]{1,0:T(4,128)S(1)} collective-permute-done((f32[4,128]{1,0:T(4,128)S(1)}, f32[4,128]{1,0:T(4,128)S(1)}, u32[]{:S(2)}, u32[]{:S(2)}) %collective-permute-start.14) | collective-permute-done | bytes 2080 | tf_op jit(solution)/shard_map/ppermute | solution.py:213
  30.0 1.7 %collective-permute-start.15 = (f32[4,128]{1,0:T(4,128)S(1)}, f32[4,128]{1,0:T(4,128)S(1)}, u32[]{:S(2)}, u32[]{:S(2)}) collective-permute-start(f32[4,128]{1,0:T(4,128)S(1)} %add.40), channel_id=1, source_target_pairs={{0,4},{4,0},{8,12},{12,8},{16,20},{20,16},{24,28},{28,24},{1,5},{5... | collective-permute-start | bytes 6152 | tf_op jit(solution)/shard_map/ppermute | solution.py:213
  31.7 1.9 %collective-permute-done.15 = f32[4,128]{1,0:T(4,128)S(1)} collective-permute-done((f32[4,128]{1,0:T(4,128)S(1)}, f32[4,128]{1,0:T(4,128)S(1)}, u32[]{:S(2)}, u32[]{:S(2)}) %collective-permute-start.15) | collective-permute-done | bytes 2080 | tf_op jit(solution)/shard_map/ppermute | solution.py:213
  33.6 1.8 %collective-permute-start.16 = (f32[4,128]{1,0:T(4,128)S(1)}, f32[4,128]{1,0:T(4,128)S(1)}, u32[]{:S(2)}, u32[]{:S(2)}) collective-permute-start(f32[4,128]{1,0:T(4,128)S(1)} %add.41), channel_id=1, source_target_pairs={{0,8},{4,12},{8,0},{12,4},{16,24},{20,28},{24,16},{28,20},{1,9},{5... | collective-permute-start | bytes 6152 | tf_op jit(solution)/shard_map/ppermute | solution.py:213
  35.4 1.8 %collective-permute-done.16 = f32[4,128]{1,0:T(4,128)S(1)} collective-permute-done((f32[4,128]{1,0:T(4,128)S(1)}, f32[4,128]{1,0:T(4,128)S(1)}, u32[]{:S(2)}, u32[]{:S(2)}) %collective-permute-start.16) | collective-permute-done | bytes 2080 | tf_op jit(solution)/shard_map/ppermute | solution.py:213
  37.2 2.8 %collective-permute-start.17 = (f32[4,128]{1,0:T(4,128)S(1)}, f32[4,128]{1,0:T(4,128)S(1)}, u32[]{:S(2)}, u32[]{:S(2)}) collective-permute-start(f32[4,128]{1,0:T(4,128)S(1)} %add.42), channel_id=1, source_target_pairs={{0,16},{4,20},{8,24},{12,28},{16,0},{20,4},{24,8},{28,12},{1,17},{... | collective-permute-start | bytes 6152 | tf_op jit(solution)/shard_map/ppermute | solution.py:213
  40.0 0.0 copy-done.1
  40.0 0.1 collective-permute-start.9
  40.1 0.0 collective-permute-done.10
  40.1 0.0 copy-done.2
  40.1 0.8 %fusion.5 = (bf16[4,128,128]{2,1,0:T(8,128)(2,1)S(1)}, f32[4,128,128]{2,1,0:T(8,128)}) fusion(bf16[4,128,128]{2,1,0:T(8,128)(2,1)S(1)} %collective-permute-done.10, f32[4,384,128]{2,1,0:T(8,128)S(1)} %copy-done.2, pred[]{:T(512)S(6)} %eq.5), kind=kLoop, calls=%fused_computation.10 | loop fusion | flops 393216 | bytes 1048577 | tf_op jit(solution)/shard_map/convert_element_type | solution.py:190
  40.9 1.5 %collective-permute-start.12 = (bf16[4,128,128]{2,1,0:T(8,128)(2,1)S(1)}, bf16[4,128,128]{2,1,0:T(8,128)(2,1)S(1)}, u32[]{:S(2)}, u32[]{:S(2)}) collective-permute-start(bf16[4,128,128]{2,1,0:T(8,128)(2,1)S(1)} %get-tuple-element.14), channel_id=1, source_target_pairs={{0,2},{1,3},{2,0},{3,1},{4,6},{5,7},{6,4},{7,5},{8,10},{9,11},{10,... | collective-permute-start | bytes 393224 | tf_op jit(solution)/shard_map/ppermute | solution.py:161
  42.4 0.0 collective-permute-done.9
  42.4 0.8 %fusion.2 = (bf16[4,128,128]{2,1,0:T(8,128)(2,1)S(1)}, f32[4,128,128]{2,1,0:T(8,128)}) fusion(bf16[4,128,128]{2,1,0:T(8,128)(2,1)S(1)} %collective-permute-done.9, f32[4,384,128]{2,1,0:T(8,128)S(1)} %copy-done.1, pred[]{:T(512)S(6)} %eq.5), kind=kLoop, calls=%fused_computation.7 | loop fusion | flops 393216 | bytes 1048577 | tf_op jit(solution)/shard_map/convert_element_type | solution.py:190
  43.2 0.5 %collective-permute-start.11 = (bf16[4,128,128]{2,1,0:T(8,128)(2,1)S(1)}, bf16[4,128,128]{2,1,0:T(8,128)(2,1)S(1)}, u32[]{:S(2)}, u32[]{:S(2)}) collective-permute-start(bf16[4,128,128]{2,1,0:T(8,128)(2,1)S(1)} %get-tuple-element.16), channel_id=1, source_target_pairs={{0,2},{1,3},{2,0},{3,1},{4,6},{5,7},{6,4},{7,5},{8,10},{9,11},{10,... | collective-permute-start | bytes 393224 | tf_op jit(solution)/shard_map/ppermute | solution.py:161
  43.7 0.0 collective-permute-done.17
  43.7 0.6 %dynamic-slice_multiply_fusion = f32[64]{0:T(128)} fusion(f32[512]{0:T(512)S(1)} %add_bitcast_fusion, s32[]{:T(128)S(6)} %select_n.63), kind=kLoop, calls=%fused_computation.18 | loop fusion | flops 64 | bytes 516 | tf_op jit(solution)/shard_map/div | solution.py:223
  44.3 2.9 %collective-permute-done.12.refs_3_ = bf16[4,128,128]{2,1,0:T(8,128)(2,1)S(1)} collective-permute-done((bf16[4,128,128]{2,1,0:T(8,128)(2,1)S(1)}, bf16[4,128,128]{2,1,0:T(8,128)(2,1)S(1)}, u32[]{:S(2)}, u32[]{:S(2)}) %collective-permute-start.12) | collective-permute-done | bytes 131104 | tf_op jit(solution)/shard_map/ppermute | solution.py:161
  47.3 0.0 copy-start.5
  47.3 2.3 %collective-permute-done.11.refs_2_ = bf16[4,128,128]{2,1,0:T(8,128)(2,1)S(1)} collective-permute-done((bf16[4,128,128]{2,1,0:T(8,128)(2,1)S(1)}, bf16[4,128,128]{2,1,0:T(8,128)(2,1)S(1)}, u32[]{:S(2)}, u32[]{:S(2)}) %collective-permute-start.11) | collective-permute-done | bytes 131104 | tf_op jit(solution)/shard_map/ppermute | solution.py:161
  49.6 0.0 copy-start.6
  49.6 0.0 copy-done.5
  49.6 0.7 %copy-done.6 = bf16[4,128,128]{2,1,0:T(8,128)(2,1)} copy-done((bf16[4,128,128]{2,1,0:T(8,128)(2,1)}, bf16[4,128,128]{2,1,0:T(8,128)(2,1)S(1)}, u32[]{:S(2)}) %copy-start.6) | copy-done | bytes 131096
  50.2 2.3 %finish.1 = (bf16[512,128]{1,0:T(8,128)(2,1)}, bf16[512,128]{1,0:T(8,128)(2,1)}) custom-call(f32[4,128,128]{2,1,0:T(8,128)} %get-tuple-element.17.refs_0_, f32[4,128,128]{2,1,0:T(8,128)} %get-tuple-element.15.refs_1_, bf16[4,128,128]{2,1,0:T(8,128)(2,1)} %copy-done.6, bf16[4,128,128]{2,1,0:T(8,128)(2,1)} %copy-done.5), custom_call_target="tpu_custom_call" | custom-call | tf_op jit(solution)/shard_map/finish/pallas_call | solution.py:201
  (7 shorter events, 0.1 us)
Async XLA Ops:
  0.6 7.5 %collective-permute-start.6 = (bf16[512,128]{1,0:T(8,128)(2,1)}, bf16[512,128]{1,0:T(8,128)(2,1)S(1)}, u32[]{:S(2)}, u32[]{:S(2)}) collective-permute-start(bf16[512,128]{1,0:T(8,128)(2,1)} %bitcast.17), channel_id=1, source_target_pairs={{0,2},{1,3},{2,0},{3,1},{4,6},{5,7},{6,4},{7,5},{8,10},{9,11},{10,... | collective-permute-start | bytes 393224 | tf_op jit(solution)/shard_map/ppermute | solution.py:161
  3.7 6.5 %collective-permute-start.7 = (bf16[512,128]{1,0:T(8,128)(2,1)}, bf16[512,128]{1,0:T(8,128)(2,1)S(1)}, u32[]{:S(2)}, u32[]{:S(2)}) collective-permute-start(bf16[512,128]{1,0:T(8,128)(2,1)} %bitcast.18), channel_id=1, source_target_pairs={{0,1},{1,0},{2,3},{3,2},{4,5},{5,4},{6,7},{7,6},{8,9},{9,8},{10,11... | collective-permute-start | bytes 393224 | tf_op jit(solution)/shard_map/ppermute | solution.py:161
  3.7 3.9 %collective-permute-start.1 = (s32[1,128]{1,0:T(1,128)}, s32[1,128]{1,0:T(1,128)S(1)}, u32[]{:S(2)}, u32[]{:S(2)}) collective-permute-start(s32[1,128]{1,0:T(1,128)} %refs_1_.1), channel_id=1, source_target_pairs={{0,2},{1,3},{2,0},{3,1},{4,6},{5,7},{6,4},{7,5},{8,10},{9,11},{10,... | collective-permute-start | bytes 1544 | tf_op jit(solution)/shard_map/ppermute | solution.py:161
  3.9 3.8 %collective-permute-start = (s32[1,128]{1,0:T(1,128)}, s32[1,128]{1,0:T(1,128)S(1)}, u32[]{:S(2)}, u32[]{:S(2)}) collective-permute-start(s32[1,128]{1,0:T(1,128)} %refs_1_.1), channel_id=1, source_target_pairs={{0,1},{1,0},{2,3},{3,2},{4,5},{5,4},{6,7},{7,6},{8,9},{9,8},{10,11... | collective-permute-start | bytes 1544 | tf_op jit(solution)/shard_map/ppermute | solution.py:161
  4.2 6.0 %collective-permute-start.3 = (bf16[512,128]{1,0:T(8,128)(2,1)}, bf16[512,128]{1,0:T(8,128)(2,1)S(1)}, u32[]{:S(2)}, u32[]{:S(2)}) collective-permute-start(bf16[512,128]{1,0:T(8,128)(2,1)} %bitcast.14), channel_id=1, source_target_pairs={{0,2},{1,3},{2,0},{3,1},{4,6},{5,7},{6,4},{7,5},{8,10},{9,11},{10,... | collective-permute-start | bytes 393224 | tf_op jit(solution)/shard_map/ppermute | solution.py:161
  7.6 4.6 %copy-start.7 = (s32[1,128]{1,0:T(1,128)}, s32[1,128]{1,0:T(1,128)S(1)}, u32[]{:S(2)}) copy-start(s32[1,128]{1,0:T(1,128)S(1)} %collective-permute-done.1.refs_3_) | copy-start | bytes 1540
  7.6 1.2 %collective-permute-start.2 = (s32[1,128]{1,0:T(1,128)S(1)}, s32[1,128]{1,0:T(1,128)S(1)}, u32[]{:S(2)}, u32[]{:S(2)}) collective-permute-start(s32[1,128]{1,0:T(1,128)S(1)} %collective-permute-done.1.refs_3_), channel_id=1, source_target_pairs={{0,1},{1,0},{2,3},{3,2},{4,5},{5,4},{6,7},{7,6},{8,9},{9,8},{10,11... | collective-permute-start | bytes 1544 | tf_op jit(solution)/shard_map/ppermute | solution.py:161
  7.6 3.3 %collective-permute-start.4 = (bf16[512,128]{1,0:T(8,128)(2,1)}, bf16[512,128]{1,0:T(8,128)(2,1)S(1)}, u32[]{:S(2)}, u32[]{:S(2)}) collective-permute-start(bf16[512,128]{1,0:T(8,128)(2,1)} %bitcast.15), channel_id=1, source_target_pairs={{0,1},{1,0},{2,3},{3,2},{4,5},{5,4},{6,7},{7,6},{8,9},{9,8},{10,11... | collective-permute-start | bytes 393224 | tf_op jit(solution)/shard_map/ppermute | solution.py:161
  8.1 4.1 %copy-start.3 = (bf16[512,128]{1,0:T(8,128)(2,1)}, bf16[512,128]{1,0:T(8,128)(2,1)S(1)}, u32[]{:S(2)}) copy-start(bf16[512,128]{1,0:T(8,128)(2,1)S(1)} %collective-permute-done.6.refs_9_) | copy-start | bytes 393220
  8.1 2.1 %collective-permute-start.8 = (bf16[512,128]{1,0:T(8,128)(2,1)S(1)}, bf16[512,128]{1,0:T(8,128)(2,1)S(1)}, u32[]{:S(2)}, u32[]{:S(2)}) collective-permute-start(bf16[512,128]{1,0:T(8,128)(2,1)S(1)} %collective-permute-done.6.refs_9_), channel_id=1, source_target_pairs={{0,1},{1,0},{2,3},{3,2},{4,5},{5,4},{6,7},{7,6},{8,9},{9,8},{10,11... | collective-permute-start | bytes 393224 | tf_op jit(solution)/shard_map/ppermute | solution.py:161
  10.2 2.0 %copy-start.4 = (bf16[512,128]{1,0:T(8,128)(2,1)}, bf16[512,128]{1,0:T(8,128)(2,1)S(1)}, u32[]{:S(2)}) copy-start(bf16[512,128]{1,0:T(8,128)(2,1)S(1)} %collective-permute-done.3.refs_6_) | copy-start | bytes 393220
  10.2 1.3 %collective-permute-start.5 = (bf16[512,128]{1,0:T(8,128)(2,1)S(1)}, bf16[512,128]{1,0:T(8,128)(2,1)S(1)}, u32[]{:S(2)}, u32[]{:S(2)}) collective-permute-start(bf16[512,128]{1,0:T(8,128)(2,1)S(1)} %collective-permute-done.3.refs_6_), channel_id=1, source_target_pairs={{0,1},{1,0},{2,3},{3,2},{4,5},{5,4},{6,7},{7,6},{8,9},{9,8},{10,11... | collective-permute-start | bytes 393224 | tf_op jit(solution)/shard_map/ppermute | solution.py:161
  12.2 12.7 %copy-start = (bf16[1,128,32,128]{3,2,1,0:T(8,128)(2,1)S(1)}, bf16[1,128,32,128]{3,2,1,0:T(8,128)(2,1)}, u32[]{:S(2)}) copy-start(bf16[1,128,32,128]{3,2,1,0:T(8,128)(2,1)} %param.8) | copy-start | bytes 3145732
  23.6 16.4 %copy-start.1 = (f32[4,384,128]{2,1,0:T(8,128)S(1)}, f32[4,384,128]{2,1,0:T(8,128)}, u32[]{:S(2)}) copy-start(f32[4,384,128]{2,1,0:T(8,128)} %get-tuple-element.10) | copy-start | bytes 2359300
  23.6 16.5 %copy-start.2 = (f32[4,384,128]{2,1,0:T(8,128)S(1)}, f32[4,384,128]{2,1,0:T(8,128)}, u32[]{:S(2)}) copy-start(f32[4,384,128]{2,1,0:T(8,128)} %get-tuple-element.11) | copy-start | bytes 2359300
  24.7 15.4 %collective-permute-start.10 = (bf16[4,128,128]{2,1,0:T(8,128)(2,1)S(1)}, bf16[4,128,128]{2,1,0:T(8,128)(2,1)S(1)}, u32[]{:S(2)}, u32[]{:S(2)}) collective-permute-start(bf16[4,128,128]{2,1,0:T(8,128)(2,1)S(1)} %slice.34), channel_id=1, source_target_pairs={{0,1},{1,0},{2,3},{3,2},{4,5},{5,4},{6,7},{7,6},{8,9},{9,8},{10,11... | collective-permute-start | bytes 393224 | tf_op jit(solution)/shard_map/ppermute | solution.py:161
  25.2 1.2 %collective-permute-start.13 = (f32[4,128]{1,0:T(4,128)S(1)}, f32[4,128]{1,0:T(4,128)S(1)}, u32[]{:S(2)}, u32[]{:S(2)}) collective-permute-start(f32[4,128]{1,0:T(4,128)S(1)} %bitcast_reduce_fusion), channel_id=1, source_target_pairs={{0,1},{1,0},{2,3},{3,2},{4,5},{5,4},{6,7},{7,6},{8,9},{9,8},{10,11... | collective-permute-start | bytes 6152 | tf_op jit(solution)/shard_map/ppermute | solution.py:213
  26.4 3.6 %collective-permute-start.14 = (f32[4,128]{1,0:T(4,128)S(1)}, f32[4,128]{1,0:T(4,128)S(1)}, u32[]{:S(2)}, u32[]{:S(2)}) collective-permute-start(f32[4,128]{1,0:T(4,128)S(1)} %add.39), channel_id=1, source_target_pairs={{0,2},{1,3},{2,0},{3,1},{4,6},{5,7},{6,4},{7,5},{8,10},{9,11},{10,... | collective-permute-start | bytes 6152 | tf_op jit(solution)/shard_map/ppermute | solution.py:213
  30.0 3.6 %collective-permute-start.15 = (f32[4,128]{1,0:T(4,128)S(1)}, f32[4,128]{1,0:T(4,128)S(1)}, u32[]{:S(2)}, u32[]{:S(2)}) collective-permute-start(f32[4,128]{1,0:T(4,128)S(1)} %add.40), channel_id=1, source_target_pairs={{0,4},{4,0},{8,12},{12,8},{16,20},{20,16},{24,28},{28,24},{1,5},{5... | collective-permute-start | bytes 6152 | tf_op jit(solution)/shard_map/ppermute | solution.py:213
  33.6 3.6 %collective-permute-start.16 = (f32[4,128]{1,0:T(4,128)S(1)}, f32[4,128]{1,0:T(4,128)S(1)}, u32[]{:S(2)}, u32[]{:S(2)}) collective-permute-start(f32[4,128]{1,0:T(4,128)S(1)} %add.41), channel_id=1, source_target_pairs={{0,8},{4,12},{8,0},{12,4},{16,24},{20,28},{24,16},{28,20},{1,9},{5... | collective-permute-start | bytes 6152 | tf_op jit(solution)/shard_map/ppermute | solution.py:213
  37.2 6.5 %collective-permute-start.17 = (f32[4,128]{1,0:T(4,128)S(1)}, f32[4,128]{1,0:T(4,128)S(1)}, u32[]{:S(2)}, u32[]{:S(2)}) collective-permute-start(f32[4,128]{1,0:T(4,128)S(1)} %add.42), channel_id=1, source_target_pairs={{0,16},{4,20},{8,24},{12,28},{16,0},{20,4},{24,8},{28,12},{1,17},{... | collective-permute-start | bytes 6152 | tf_op jit(solution)/shard_map/ppermute | solution.py:213
  40.0 2.4 %collective-permute-start.9 = (bf16[4,128,128]{2,1,0:T(8,128)(2,1)S(1)}, bf16[4,128,128]{2,1,0:T(8,128)(2,1)S(1)}, u32[]{:S(2)}, u32[]{:S(2)}) collective-permute-start(bf16[4,128,128]{2,1,0:T(8,128)(2,1)S(1)} %slice.35), channel_id=1, source_target_pairs={{0,1},{1,0},{2,3},{3,2},{4,5},{5,4},{6,7},{7,6},{8,9},{9,8},{10,11... | collective-permute-start | bytes 393224 | tf_op jit(solution)/shard_map/ppermute | solution.py:161
  40.9 6.4 %collective-permute-start.12 = (bf16[4,128,128]{2,1,0:T(8,128)(2,1)S(1)}, bf16[4,128,128]{2,1,0:T(8,128)(2,1)S(1)}, u32[]{:S(2)}, u32[]{:S(2)}) collective-permute-start(bf16[4,128,128]{2,1,0:T(8,128)(2,1)S(1)} %get-tuple-element.14), channel_id=1, source_target_pairs={{0,2},{1,3},{2,0},{3,1},{4,6},{5,7},{6,4},{7,5},{8,10},{9,11},{10,... | collective-permute-start | bytes 393224 | tf_op jit(solution)/shard_map/ppermute | solution.py:161
  43.2 6.4 %collective-permute-start.11 = (bf16[4,128,128]{2,1,0:T(8,128)(2,1)S(1)}, bf16[4,128,128]{2,1,0:T(8,128)(2,1)S(1)}, u32[]{:S(2)}, u32[]{:S(2)}) collective-permute-start(bf16[4,128,128]{2,1,0:T(8,128)(2,1)S(1)} %get-tuple-element.16), channel_id=1, source_target_pairs={{0,2},{1,3},{2,0},{3,1},{4,6},{5,7},{6,4},{7,5},{8,10},{9,11},{10,... | collective-permute-start | bytes 393224 | tf_op jit(solution)/shard_map/ppermute | solution.py:161
  47.3 2.3 %copy-start.5 = (bf16[4,128,128]{2,1,0:T(8,128)(2,1)}, bf16[4,128,128]{2,1,0:T(8,128)(2,1)S(1)}, u32[]{:S(2)}) copy-start(bf16[4,128,128]{2,1,0:T(8,128)(2,1)S(1)} %collective-permute-done.12.refs_3_) | copy-start | bytes 393220
  49.6 0.7 %copy-start.6 = (bf16[4,128,128]{2,1,0:T(8,128)(2,1)}, bf16[4,128,128]{2,1,0:T(8,128)(2,1)S(1)}, u32[]{:S(2)}) copy-start(bf16[4,128,128]{2,1,0:T(8,128)(2,1)S(1)} %collective-permute-done.11.refs_2_) | copy-start | bytes 393220
